TPU v7x, 32 devices: a whole 2x2x4 slice. The times are simulated.
32 devices in a mesh: gx: 4 (over z), gy: 8 (over y, x, core).
Axes of the slice: x: 2, y: 2, z: 4, core: 2. Of those that a mesh axis runs over, the one named last changes fastest.
Arguments:
- centres: bfloat16 [131072, 256], P(('gx', 'gy')), may hold values from -20 to 20
- weights: float32 [16, 131072], P(None, ('gx', 'gy')), may hold values from -1 to 1
- targets: float32 [16, 256], P(None, ('gx', 'gy')), may hold values from -6 to 6
- batch_index: int32 [256], P(('gx', 'gy')), may hold values from 0 to 131071, as said below
- nystrom_index: int32 [2048], P(('gx', 'gy')), may hold values from 0 to 131071, as said below
- eigvecs: float32 [2048, 128], P(('gx', 'gy')), may hold values from -0.125 to 0.125
- scales: float32 [128], replicated, may hold values from 0.2 to 2
Outputs:
- residual: float32 [16, 256], P(None, ('gx', 'gy'))
- block_correction: float32 [16, 2048], P(None, ('gx', 'gy'))
Inputs may be any that keep to these rules, and one draw needn't show every extreme that they name: `batch_index`: the entries at positions j * 8 to (j + 1) * 8 - 1 name centres j * 4096 to (j + 1) * 4096 - 1, all different. `nystrom_index`: the entries at positions j * 64 to (j + 1) * 64 - 1 name centres j * 4096 to (j + 1) * 4096 - 1, all different.
All inputs are finite; a program needn't handle non-finite values.
Results may differ from a plain program's by a relative error of at most 0.0003.
Values may be sent and summed in bfloat16 or wider, within the bound.
A program may use at most 192 MiB of HBM per device.

v0:
```python
import jax
import jax.numpy as jnp
from jax import lax
from jax.sharding import PartitionSpec as P


def kernel_tile(points, point_norm, others, other_norm):
    width = float(points.shape[1]) ** 0.5
    inner = jnp.dot(points, others.T, preferred_element_type=jnp.float32)
    squared = point_norm[:, None] + other_norm[None, :] - 2.0 * inner
    return jnp.exp(-jnp.sqrt(jnp.maximum(squared, 1.0)) / width)


def combine_projection(partial_projection):
    return lax.psum(partial_projection, ("gx", "gy"))


def on_device(centres, weights, targets, batch_index, nystrom_index, eigvecs, scales):
    device_rank = lax.axis_index(("gx", "gy"))
    local_count = centres.shape[0]
    outputs = weights.shape[0]
    local_batch = batch_index - device_rank * local_count
    local_block = nystrom_index - device_rank * local_count
    batch_local = jnp.take(centres, local_batch, axis=0)
    centre_norm = jnp.sum(centres.astype(jnp.float32) ** 2, axis=1)
    rows_in = lax.all_gather(batch_local, ("gx", "gy"), axis=0, tiled=True)
    rows_norm = jnp.sum(rows_in.astype(jnp.float32) ** 2, axis=1)
    tile = kernel_tile(rows_in, rows_norm, centres, centre_norm)
    predicted = lax.dot_general(
        weights, tile, (((1,), (1,)), ((), ())), precision=lax.Precision.HIGHEST
    )
    block_tile = jnp.take(tile, local_block, axis=1)
    carried = block_tile.T
    gathered = jnp.concatenate([predicted, carried], axis=0)
    partial_prediction = gathered[:outputs]
    carried = gathered[outputs:]
    inner_sum = lax.psum(partial_prediction, "gy")
    reduced = lax.psum(inner_sum, "gx")
    targets_full = lax.all_gather(targets, ("gx", "gy"), axis=1, tiled=True)
    residual_full = reduced - targets_full
    residual_local = lax.dynamic_slice_in_dim(
        residual_full, device_rank * batch_local.shape[0], batch_local.shape[0], 1
    )
    along = jnp.dot(carried, residual_full.T, precision=lax.Precision.HIGHEST)
    projection = combine_projection(jnp.dot(eigvecs.T, along, precision=lax.Precision.HIGHEST))
    correction = jnp.dot(eigvecs * scales[None, :], projection, precision=lax.Precision.HIGHEST)
    return (residual_local, correction.T)


def solution(mesh):
    return jax.shard_map(
        on_device,
        mesh=mesh,
        in_specs=(
            P(("gx", "gy"), None),
            P(None, ("gx", "gy")),
            P(None, ("gx", "gy")),
            P(("gx", "gy")),
            P(("gx", "gy")),
            P(("gx", "gy"), None),
            P(),
        ),
        out_specs=(P(None, ("gx", "gy")), P(None, ("gx", "gy"))),
        check_vma=False,
    )
```

profile of v0, /device:TPU:0, one launch (start us, length us, event | category | flops | bytes accessed | tf_op | source)
XLA Modules:
  0.0 181.4 jit_solution(13803542961892802203)
XLA Ops:
  0.6 0.0 copy-start
  0.7 0.7 compare_and_fusion.1
  1.4 2.4 %gather_fusion = bf16[8,256]{1,0:T(8,128)(2,1)S(1)} fusion(bf16[4096,256]{1,0:T(8,128)(2,1)} %param.7, s32[1024]{0:T(1024)S(1)} %pad_clamp_fusion.1), kind=kCustom, calls=%fused_computation | custom fusion | bytes 8224 | tf_op jit(solution)/shard_map/jit(_take)/gather | solution.py:24
  3.8 0.1 broadcast_select_fusion
  3.9 43.6 %all_gather.6 = bf16[256,256]{1,0:T(8,128)(2,1)S(1)} all-gather(bf16[8,256]{1,0:T(8,128)(2,1)S(1)} %broadcast_select_fusion), channel_id=1, replica_groups=mesh['gx'=4,'gy'=8] {'gx','gy'}, dimensions={0}, use_global_device_ids=true | all-gather | bytes 135168 | tf_op jit(solution)/shard_map/all_gather | solution.py:26
  47.4 2.2 %multiply_reduce_fusion = f32[4096]{0:T(1024)S(1)} fusion(bf16[4096,256]{1,0:T(8,128)(2,1)} %param.7), kind=kLoop, calls=%fused_computation.9 | loop fusion | flops 3141632 | bytes 2113536 | tf_op jit(solution)/shard_map/reduce_sum | solution.py:25
  49.7 0.1 multiply_reduce_fusion.1
  49.8 3.8 %fusion.5 = f32[256,4096]{1,0:T(8,128)S(1)} fusion(bf16[256,256]{1,0:T(8,128)(2,1)S(1)} %all_gather.6, bf16[4096,256]{1,0:T(8,128)(2,1)} %param.7, f32[4096]{0:T(1024)S(1)} %multiply_reduce_fusion, f32[256]{0:T(256)S(1)} %multiply_reduce_fusion.1), kind=kOutput, calls=%fused_computation.8 | convolution fusion | flops 543162368 | bytes 6439936 | tf_op jit(solution)/shard_map/dot_general | solution.py:9
  53.6 0.0 copy-start.1
  53.6 1.9 %copy-done.1 = f32[256,4096]{1,0:T(8,128)} copy-done((f32[256,4096]{1,0:T(8,128)}, f32[256,4096]{1,0:T(8,128)S(1)}, u32[]{:S(2)}) %copy-start.1) | copy-done | bytes 4194328
  55.5 3.3 %convolution_bitcast_fusion = f32[16,256]{1,0:T(8,128)S(1)} fusion(f32[256,4096]{1,0:T(8,128)S(1)} %fusion.5, f32[16,4096]{1,0:T(8,128)S(1)} %copy-done), kind=kOutput, calls=%fused_computation.10 | convolution fusion | flops 201326592 | bytes 4472832 | tf_op jit(solution)/shard_map/dot_general | solution.py:29
  58.9 22.5 %psum.21 = f32[16,256]{1,0:T(8,128)S(1)} all-reduce(f32[16,256]{1,0:T(8,128)S(1)} %convolution_bitcast_fusion), channel_id=1, replica_groups=mesh['gx'=4,'gy'=8] {'gy'}, use_global_device_ids=true, to_apply=%region_2.3 | all-reduce | flops 4096 | bytes 32768 | tf_op jit(solution)/shard_map/psum | solution.py:37
  81.4 15.5 %psum.22 = f32[16,256]{1,0:T(8,128)S(1)} all-reduce(f32[16,256]{1,0:T(8,128)S(1)} %psum.21), channel_id=1, replica_groups=mesh['gx'=4,'gy'=8] {'gx'}, use_global_device_ids=true, to_apply=%region_3.4 | all-reduce | flops 4096 | bytes 32768 | tf_op jit(solution)/shard_map/psum | solution.py:38
  96.9 36.7 %all_gather.7 = f32[16,256]{0,1:T(8,128)S(1)} all-gather(f32[16,8]{0,1:T(8,128)S(1)} %copy-done.3), channel_id=1, replica_groups=mesh['gx'=4,'gy'=8] {'gx','gy'}, dimensions={1}, use_global_device_ids=true | all-gather | bytes 16896 | tf_op jit(solution)/shard_map/all_gather | solution.py:39
  133.6 0.1 copy.12
  133.7 0.1 constant_dynamic-slice_fusion
  133.7 0.7 copy.14
  134.4 5.6 %copy.13 = f32[256,4096]{0,1:T(8,128)} copy(f32[256,4096]{1,0:T(8,128)} %copy-done.1) | data formatting | bytes 8388608 | tf_op jit(solution)/shard_map/exp | solution.py:11
  140.1 2.8 %gather_fusion.1 = f32[64,256]{1,0:T(8,128)S(1)} fusion(f32[256,4096]{0,1:T(8,128)} %copy.13, s32[1024]{0:T(1024)S(1)} %pad_clamp_fusion), kind=kCustom, calls=%fused_computation.1 | custom fusion | bytes 131328 | tf_op jit(solution)/shard_map/jit(_take)/gather | solution.py:32
  142.9 0.3 fusion.6
  143.2 0.0 copy-done.2
  143.2 0.2 convolution_bitcast_fusion.1
  143.4 37.3 %psum.23 = f32[128,16]{0,1:T(8,128)S(1)} all-reduce(f32[128,16]{0,1:T(8,128)S(1)} %convolution_bitcast_fusion.1), channel_id=1, replica_groups=mesh['gx'=4,'gy'=8] {'gx','gy'}, use_global_device_ids=true, to_apply=%region_4.5 | all-reduce | flops 2048 | bytes 16384 | tf_op jit(solution)/shard_map/psum | solution.py:15
  180.6 0.8 fusion.9
  (12 shorter events, 0.0 us)
Async XLA Ops:
  0.6 54.9 %copy-start = (f32[16,4096]{1,0:T(8,128)S(1)}, f32[16,4096]{1,0:T(8,128)}, u32[]{:S(2)}) copy-start(f32[16,4096]{1,0:T(8,128)} %param.8) | copy-start | bytes 786436
  53.6 1.9 %copy-start.1 = (f32[256,4096]{1,0:T(8,128)}, f32[256,4096]{1,0:T(8,128)S(1)}, u32[]{:S(2)}) copy-start(f32[256,4096]{1,0:T(8,128)S(1)} %fusion.5) | copy-start | bytes 12582916
  55.5 41.4 %copy-start.3 = (f32[16,8]{0,1:T(8,128)S(1)}, f32[16,8]{0,1:T(8,128)}, u32[]{:S(2)}) copy-start(f32[16,8]{0,1:T(8,128)} %param.9) | copy-start | bytes 1540
  134.4 5.6 %copy-start.5 = (s32[64]{0:T(128)S(1)}, s32[64]{0:T(128)}, u32[]{:S(2)}) copy-start(s32[64]{0:T(128)} %param.11) | copy-start | bytes 772
  134.4 8.8 %copy-start.2 = (f32[64,128]{1,0:T(8,128)S(1)}, f32[64,128]{1,0:T(8,128)}, u32[]{:S(2)}) copy-start(f32[64,128]{1,0:T(8,128)} %param.12) | copy-start | bytes 98308
  134.4 46.2 %copy-start.4 = (f32[128]{0:T(128)S(1)}, f32[128]{0:T(128)}, u32[]{:S(2)}) copy-start(f32[128]{0:T(128)} %param.13) | copy-start | bytes 1540
where the time goes:
time: 183 us; the launch traced here: 181 us
  blocking collectives  156 us (85%)
  local copies, waits for them, and re-layouts  13.7 us (7%)
  matrix products  8.4 us (5%)
  other arithmetic  3.13 us (2%)
    all_gather x1, blocking collectives, on_device(): rows_in = lax.all_gather(batch_local, ('gx', 'gy'), axis=0, tiled=True)  43.6 us
    psum x1, blocking collectives, combine_projection(): return lax.psum(partial_projection, ('gx', 'gy'))  37.3 us
    all_gather x1, blocking collectives, on_device(): targets_full = lax.all_gather(targets, ('gx', 'gy'), axis=1, tiled=True)  36.7 us
    psum x1, blocking collectives, on_device(): inner_sum = lax.psum(partial_prediction, 'gy')  22.5 us
    psum x1, blocking collectives, on_device(): reduced = lax.psum(inner_sum, 'gx')  15.5 us
    exp x1, local copies, waits for them, and re-layouts, kernel_tile(): return jnp.exp(-jnp.sqrt(jnp.maximum(squared, 1.0)) / width)  5.64 us
    dot_general x1, matrix products, kernel_tile(): inner = jnp.dot(points, others.T, preferred_element_type=jnp.float32)  3.82 us

commit v1 on v0

v1 whole, which is shorter than its diff:
```python
import functools
import math

import jax
import jax.numpy as jnp
from jax import lax
from jax.experimental import pallas as pl
from jax.experimental.pallas import tpu as pltpu
from jax.sharding import PartitionSpec as P

F32 = jnp.float32
BF16 = jnp.bfloat16
HIGHEST = lax.Precision.HIGHEST
NT = (((1,), (1,)), ((), ()))
MESH = pl.DeviceIdType.MESH


def nt(a, b, precision=None):
    return lax.dot_general(a, b, NT, precision=precision, preferred_element_type=F32)


def split(x):
    high = x.astype(BF16)
    return high, (x - high.astype(F32)).astype(BF16)


def kernel(
    nx, ny,
    bidx, nidx, targets, eig, scales, weights_hbm, centres_hbm,
    res_out, corr_out,
    cen, wv, w2, nj, rows_buf, rowsm, nb, acc, khi, klo,
    mt_loc, mt_recv, mt_all, p_loc, p_recv, r_all,
    cen_sem, w_sem, send_sems, recv_sems,
):
    n = nx * ny
    gx, gy = lax.axis_index("gx"), lax.axis_index("gy")
    me = gx * ny + gy
    count, dim = cen.shape
    outputs = wv.shape[0]
    per = rows_buf.shape[1]
    batch = n * per
    lanes = per * outputs
    block = eig.shape[0]
    step_j = khi.shape[1]
    step_b = khi.shape[0]
    rate = -math.log2(math.e) / float(dim) ** 0.5

    cen_copies = []
    parts = cen_sem.shape[0]
    size = count // parts
    for part in range(parts):
        at = pl.ds(part * size, size)
        copy = pltpu.make_async_copy(centres_hbm.at[at], cen.at[at], cen_sem.at[part])
        copy.start()
        cen_copies.append(copy)
    w_copy = pltpu.make_async_copy(weights_hbm, wv, w_sem)
    w_copy.start()

    barrier = pltpu.get_barrier_semaphore()

    def other(k):
        t = lax.rem(me + k, n)
        return t, (lax.div(t, ny), lax.rem(t, ny))

    def greet(k, carry):
        _, where = other(k)
        pl.semaphore_signal(barrier, inc=1, device_id=where, device_id_type=MESH)
        return carry

    lax.fori_loop(1, n, greet, 0)

    def send_all(phase, source, target):
        def one(k, carry):
            t, where = other(k)
            pltpu.make_async_remote_copy(
                src_ref=source(t), dst_ref=target.at[me],
                send_sem=send_sems.at[phase], recv_sem=recv_sems.at[phase],
                device_id=where, device_id_type=MESH,
            ).start()
            return carry

        lax.fori_loop(1, n, one, 0)

    def wait_bytes(buf, sem):
        view = buf.at[pl.ds(0, n - 1)]
        pltpu.make_async_copy(view, view, sem).wait()

    first = me * count

    def column(ref):
        length = ref.shape[1]
        local = (ref[...] - first).astype(F32)
        row = lax.broadcasted_iota(jnp.int32, (length, length), 0)
        col = lax.broadcasted_iota(jnp.int32, (length, length), 1)
        return jnp.sum(jnp.where(row == col, local, 0.0), axis=1, keepdims=True)

    wanted = jnp.concatenate([column(bidx), column(nidx)], axis=0)
    picked = jnp.zeros((per + block, dim), F32)
    for part in range(parts):
        cen_copies[part].wait()
        spot = lax.broadcasted_iota(jnp.int32, (per + block, size), 1) + part * size
        hot = jnp.where(spot.astype(F32) == wanted, 1.0, 0.0).astype(BF16)
        picked = picked + jnp.dot(hot, cen[part * size:(part + 1) * size, :], preferred_element_type=F32)
    rows_buf[me] = picked[:per].astype(BF16)
    pl.semaphore_wait(barrier, n - 1)
    send_all(0, lambda t: rows_buf.at[me], rows_buf)

    blk = picked[per:]
    ones_f = jnp.ones((8, dim), F32)
    blk_norm = nt(ones_f, blk * blk, HIGHEST)[:1]
    blk = blk.astype(BF16)
    ones_b = jnp.ones((8, dim), BF16)

    def norms(i, carry):
        at = pl.ds(pl.multiple_of(i * 512, 512), 512)
        v = cen[at, :].astype(F32)
        high, low = split(v * v)
        nj[:, at] = nt(ones_b, high) + nt(ones_b, low)
        return carry

    lax.fori_loop(0, count // 512, norms, 0)
    w_copy.wait()
    whigh, wlow = split(wv[...])
    for rep in range(per):
        w2[rep * outputs:(rep + 1) * outputs, :] = whigh
        w2[lanes + rep * outputs:lanes + (rep + 1) * outputs, :] = wlow
    scaled = eig[...] * scales[...]
    o_row = lax.broadcasted_iota(jnp.int32, (outputs, lanes), 0)
    o_col = lax.broadcasted_iota(jnp.int32, (outputs, lanes), 1)
    o_mask = jnp.where(lax.rem(o_col, outputs) == o_row, 1.0, 0.0)
    b_row = lax.broadcasted_iota(jnp.int32, (per, lanes), 0)
    b_col = lax.broadcasted_iota(jnp.int32, (per, lanes), 1)
    b_mask = jnp.where(lax.div(b_col, outputs) == b_row, 1.0, 0.0)
    tgt = jnp.dot(targets[...], b_mask, precision=HIGHEST, preferred_element_type=F32)
    tgt = jnp.sum(tgt * o_mask, axis=0, keepdims=True)

    wait_bytes(rows_buf, recv_sems.at[0])
    rows = rows_buf[...].astype(F32).reshape(batch, dim)
    row_norm = jnp.sum(rows * rows, axis=1, keepdims=True)
    nb[...] = jnp.broadcast_to(row_norm, nb.shape)
    rowsm[...] = (rows * -2.0).astype(BF16)

    def kern(total):
        total = jnp.maximum(total, 1.0)
        return jnp.exp2(total * lax.rsqrt(total) * rate)

    block_tile = kern(nt(rowsm[...], blk) + (row_norm + blk_norm))
    mt = jnp.dot(block_tile, eig[...], precision=HIGHEST, preferred_element_type=F32)
    mt_loc[...] = mt.reshape(mt_loc.shape)
    send_all(1, lambda t: mt_loc.at[t], mt_recv)
    mt_recv[me] = mt_loc[me]

    acc[...] = jnp.zeros_like(acc)

    def main_b(bi, carry):
        at_b = pl.ds(pl.multiple_of(bi * step_b, step_b), step_b)

        def main_j(ji, carry):
            for sub in range(step_j // 256):
                at = pl.ds(pl.multiple_of(ji * step_j + sub * 256, 256), 256)
                norm = jnp.concatenate([nb[at_b, :]] * (256 // nb.shape[1]), axis=1)
                tile = kern(nt(rowsm[at_b, :], cen[at, :]) + (norm + nj[:1, at]))
                high, low = split(tile)
                khi[:, sub * 256:(sub + 1) * 256] = high
                klo[:, sub * 256:(sub + 1) * 256] = low
            at = pl.ds(pl.multiple_of(ji * step_j, step_j), step_j)
            acc[at_b, :] += nt(khi[...], w2[:, at]) + nt(klo[...], w2[:, at])
            return carry

        return lax.fori_loop(0, count // step_j, main_j, carry)

    lax.fori_loop(0, batch // step_b, main_b, 0)
    both = acc[:, :lanes] + acc[:, lanes:]
    p_loc[...] = jnp.sum(both.reshape(n, per, lanes) * b_mask[None], axis=1, keepdims=True)
    send_all(2, lambda t: p_loc.at[t], p_recv)
    p_recv[me] = p_loc[me]

    wait_bytes(mt_recv, recv_sems.at[1])
    mt_all[me] = jnp.sum(mt_recv[...], axis=0)
    send_all(3, lambda t: mt_all.at[me], mt_all)

    wait_bytes(p_recv, recv_sems.at[2])
    mine = jnp.sum(p_recv[...], axis=0) - tgt
    r_all[me] = mine
    send_all(4, lambda t: r_all.at[me], r_all)
    res_out[...] = nt(mine * o_mask, b_mask, HIGHEST)

    wait_bytes(mt_all, recv_sems.at[3])
    carry_n = nt(scaled, mt_all[...].reshape(batch, scaled.shape[1]), HIGHEST)
    wait_bytes(r_all, recv_sems.at[4])
    spread = (r_all[...] * b_mask[None]).reshape(batch, lanes)
    wide = jnp.dot(carry_n, spread, precision=HIGHEST, preferred_element_type=F32)
    corr_out[...] = nt(o_mask, wide, HIGHEST)

    wait_bytes(rows_buf, send_sems.at[0])
    wait_bytes(mt_loc, send_sems.at[1])
    wait_bytes(p_loc, send_sems.at[2])
    wait_bytes(mt_all, send_sems.at[3])
    wait_bytes(r_all, send_sems.at[4])


def on_device(nx, ny, centres, weights, targets, batch_index, nystrom_index, eigvecs, scales):
    n = nx * ny
    count, dim = centres.shape
    outputs = weights.shape[0]
    per = batch_index.shape[0]
    block = nystrom_index.shape[0]
    eigen = eigvecs.shape[1]
    lanes = per * outputs
    batch = n * per
    step_j = min(count, 1024)
    step_b = min(batch, 256)
    vmem = pl.BlockSpec(memory_space=pltpu.VMEM)
    hbm = pl.BlockSpec(memory_space=pl.ANY)
    return pl.pallas_call(
        functools.partial(kernel, nx, ny),
        out_shape=(
            jax.ShapeDtypeStruct((outputs, per), F32),
            jax.ShapeDtypeStruct((outputs, block), F32),
        ),
        in_specs=[vmem] * 5 + [hbm] * 2,
        out_specs=(vmem, vmem),
        scratch_shapes=[
            pltpu.VMEM((count, dim), BF16),
            pltpu.VMEM((outputs, count), F32),
            pltpu.VMEM((2 * lanes, count), BF16),
            pltpu.VMEM((8, count), F32),
            pltpu.VMEM((n, per, dim), BF16),
            pltpu.VMEM((batch, dim), BF16),
            pltpu.VMEM((batch, 128), F32),
            pltpu.VMEM((batch, 2 * lanes), F32),
            pltpu.VMEM((step_b, step_j), BF16),
            pltpu.VMEM((step_b, step_j), BF16),
            pltpu.VMEM((n, per, eigen), F32),
            pltpu.VMEM((n, per, eigen), F32),
            pltpu.VMEM((n, per, eigen), F32),
            pltpu.VMEM((n, 1, lanes), F32),
            pltpu.VMEM((n, 1, lanes), F32),
            pltpu.VMEM((n, 1, lanes), F32),
            pltpu.SemaphoreType.DMA((4,)),
            pltpu.SemaphoreType.DMA,
            pltpu.SemaphoreType.DMA((5,)),
            pltpu.SemaphoreType.DMA((5,)),
        ],
        compiler_params=pltpu.CompilerParams(
            collective_id=0, has_side_effects=True, vmem_limit_bytes=60 * 1024 * 1024
        ),
    )(
        batch_index.reshape(1, per), nystrom_index.reshape(1, block), targets, eigvecs,
        scales.reshape(1, eigen), weights, centres,
    )


def solution(mesh):
    return jax.shard_map(
        functools.partial(on_device, mesh.shape["gx"], mesh.shape["gy"]),
        mesh=mesh,
        in_specs=(
            P(("gx", "gy"), None),
            P(None, ("gx", "gy")),
            P(None, ("gx", "gy")),
            P(("gx", "gy")),
            P(("gx", "gy")),
            P(("gx", "gy"), None),
            P(),
        ),
        out_specs=(P(None, ("gx", "gy")), P(None, ("gx", "gy"))),
        check_vma=False,
    )
```

time: 183 us -> 31.6 us (0.17)
  blocking collectives: 156 us -> 0 us
  Pallas kernels: 0 us -> 26.6 us
  local copies, waits for them, and re-layouts: 13.7 us -> 4.01 us
  matrix products: 8.4 us -> 0 us
  other arithmetic: 3.13 us -> 0 us
    all_gather x2 -> x0, blocking collectives: 80.2 us -> none  [the longest x1 43.6 us: on_device(): rows_in = lax.all_gather(batch_local, ('gx', 'gy'), axis=0, tiled=True)]
    psum x3 -> x0, blocking collectives: 75.3 us -> none  [the longest x1 37.3 us: combine_projection(): return lax.psum(partial_projection, ('gx', 'gy'))]
    pallas_call x0 -> x1, Pallas kernels: none -> 26.6 us  [on_device(): pl.pallas_call(functools.partial(kernel, nx, ny), out_shape=(jax.ShapeDty...]
    dot_general x5 -> x0, matrix products: 8.4 us -> none  [the longest x1 3.82 us: kernel_tile(): inner = jnp.dot(points, others.T, preferred_element_type=jnp.float32)]
    exp x1 -> x0, local copies, waits for them, and re-layouts: 5.64 us -> none  [kernel_tile(): return jnp.exp(-jnp.sqrt(jnp.maximum(squared, 1.0)) / width)]
    gather x2 -> x0, local copies, waits for them, and re-layouts: 5.27 us -> none  [the longest x1 2.84 us: on_device(): block_tile = jnp.take(tile, local_block, axis=1)]
    reduce_sum x2 -> x0, other arithmetic: 2.32 us -> none  [the longest x1 2.21 us: on_device(): centre_norm = jnp.sum(centres.astype(jnp.float32) ** 2, axis=1)]
where the time goes in v1:
time: 31.6 us; the launch traced here: 31.2 us
  Pallas kernels  26.6 us (84%)
  local copies, waits for them, and re-layouts  4.01 us (13%)
  between operations  0.64 us (2%)
    pallas_call x1, Pallas kernels, on_device(): pl.pallas_call(functools.partial(kernel, nx, ny), out_shape=(jax.ShapeDty...  26.6 us
    unnamed x2, local copies, waits for them, and re-layouts  2.65 us
    pallas_call x1, local copies, waits for them, and re-layouts, on_device(): pl.pallas_call(functools.partial(kernel, nx, ny), out_shape=(jax.ShapeDty...  1.36 us

profile of v1, /device:TPU:0, one launch (start us, length us, event | category | flops | bytes accessed | tf_op | source)
XLA Modules:
  0.0 31.2 jit_solution(2887394726317599431)
XLA Ops:
  0.6 1.4 %copy.9.targets = f32[16,8]{1,0:T(8,128)} copy(f32[16,8]{0,1:T(8,128)} %param.9) | data formatting | bytes 1024 | tf_op args[2]
  2.0 26.6 %shard_map.86 = (f32[16,8]{1,0:T(8,128)}, f32[16,64]{1,0:T(8,128)}) custom-call(s32[1,8]{1,0:T(1,128)} %bitcast.3, s32[1,64]{1,0:T(1,128)} %bitcast.4, f32[16,8]{1,0:T(8,128)} %copy.9.targets, f32[64,128]{1,0:T(8,128)} %eig.1, f32[1,128]{1,0:T(1,128)} %bitcast.5, f32[16,4096]{1,0:T(8,128)} %weights_hbm.1, bf16[4096,256]{1,0:T(8,128)(2,1)} %centres_hbm.1), custom_call_target="tpu_custom_call" | custom-call | tf_op jit(solution)/shard_map/pallas_call | solution.py:215
  28.6 1.4 %copy.10 = f32[16,8]{0,1:T(8,128)} copy(f32[16,8]{1,0:T(8,128)} %get-tuple-element.2) | data formatting | bytes 1024 | tf_op jit(solution)/shard_map/pallas_call | solution.py:215
  30.0 1.3 %copy.12 = f32[16,64]{1,0:T(8,128)} copy(f32[16,64]{1,0:T(8,128)} %get-tuple-element.7) | data formatting | bytes 8192

commit v2 on v1

--- a/solution.py
+++ b/solution.py
@@ -131,8 +131,8 @@
     b_row = lax.broadcasted_iota(jnp.int32, (per, lanes), 0)
     b_col = lax.broadcasted_iota(jnp.int32, (per, lanes), 1)
     b_mask = jnp.where(lax.div(b_col, outputs) == b_row, 1.0, 0.0)
-    tgt = jnp.dot(targets[...], b_mask, precision=HIGHEST, preferred_element_type=F32)
-    tgt = jnp.sum(tgt * o_mask, axis=0, keepdims=True)
+    tgt = jnp.dot(targets[...], o_mask, precision=HIGHEST, preferred_element_type=F32)
+    tgt = jnp.sum(tgt * b_mask, axis=0, keepdims=True)
 
     wait_bytes(rows_buf, recv_sems.at[0])
     rows = rows_buf[...].astype(F32).reshape(batch, dim)
@@ -183,7 +183,7 @@
     mine = jnp.sum(p_recv[...], axis=0) - tgt
     r_all[me] = mine
     send_all(4, lambda t: r_all.at[me], r_all)
-    res_out[...] = nt(mine * o_mask, b_mask, HIGHEST)
+    res_out[...] = nt(mine * b_mask, o_mask, HIGHEST)
 
     wait_bytes(mt_all, recv_sems.at[3])
     carry_n = nt(scaled, mt_all[...].reshape(batch, scaled.shape[1]), HIGHEST)
@@ -197,6 +197,11 @@
     wait_bytes(p_loc, send_sems.at[2])
     wait_bytes(mt_all, send_sems.at[3])
     wait_bytes(r_all, send_sems.at[4])
+
+
+def hand_out(res_in, corr_in, res_out, corr_out):
+    res_out[...] = res_in[...]
+    corr_out[...] = corr_in[...]
 
 
 def on_device(nx, ny, centres, weights, targets, batch_index, nystrom_index, eigvecs, scales):
@@ -212,10 +217,10 @@
     step_b = min(batch, 256)
     vmem = pl.BlockSpec(memory_space=pltpu.VMEM)
     hbm = pl.BlockSpec(memory_space=pl.ANY)
-    return pl.pallas_call(
+    res, corr = pl.pallas_call(
         functools.partial(kernel, nx, ny),
         out_shape=(
-            jax.ShapeDtypeStruct((outputs, per), F32),
+            jax.ShapeDtypeStruct((per, outputs), F32),
             jax.ShapeDtypeStruct((outputs, block), F32),
         ),
         in_specs=[vmem] * 5 + [hbm] * 2,
@@ -246,9 +251,16 @@
             collective_id=0, has_side_effects=True, vmem_limit_bytes=60 * 1024 * 1024
         ),
     )(
-        batch_index.reshape(1, per), nystrom_index.reshape(1, block), targets, eigvecs,
+        batch_index.reshape(1, per), nystrom_index.reshape(1, block), targets.T, eigvecs,
         scales.reshape(1, eigen), weights, centres,
     )
+    res, corr = pl.pallas_call(
+        hand_out,
+        out_shape=(jax.ShapeDtypeStruct(res.shape, F32), jax.ShapeDtypeStruct(corr.shape, F32)),
+        in_specs=[vmem] * 2,
+        out_specs=(vmem, vmem),
+    )(res, corr)
+    return res.T, corr
 
 
 def solution(mesh):

time: 31.6 us -> 28.7 us (0.908)
  local copies, waits for them, and re-layouts: 4.01 us -> 0 us
  Pallas kernels: 26.6 us -> 27.8 us
    unnamed x2 -> x0, local copies, waits for them, and re-layouts: 2.65 us -> none
    pallas_call x1 -> x0, local copies, waits for them, and re-layouts: 1.36 us -> none  [on_device(): pl.pallas_call(functools.partial(kernel, nx, ny), out_shape=(jax.ShapeDty...]
    pallas_call x0 -> x1, Pallas kernels: none -> 1.31 us  [on_device(): pl.pallas_call(hand_out, out_shape=(jax.ShapeDtypeStruct(res.shape, F32),...]
where the time goes in v2:
time: 28.7 us; the launch traced here: 28.5 us
  Pallas kernels  27.8 us (97%)
  between operations  0.64 us (2%)
    pallas_call x1, Pallas kernels, on_device(): pl.pallas_call(functools.partial(kernel, nx, ny), out_shape=(jax.ShapeDty...  26.5 us
    pallas_call x1, Pallas kernels, on_device(): pl.pallas_call(hand_out, out_shape=(jax.ShapeDtypeStruct(res.shape, F32),...  1.31 us

profile of v2, /device:TPU:0, one launch (start us, length us, event | category | flops | bytes accessed | tf_op | source)
XLA Modules:
  0.0 28.5 jit_solution(2963389072670860412)
XLA Ops:
  0.6 26.5 %shard_map.86 = (f32[8,16]{1,0:T(8,128)}, f32[16,64]{1,0:T(8,128)}) custom-call(s32[1,8]{1,0:T(1,128)} %bitcast.6, s32[1,64]{1,0:T(1,128)} %bitcast.7, f32[8,16]{1,0:T(8,128)} %bitcast.5, f32[64,128]{1,0:T(8,128)} %eig.1, f32[1,128]{1,0:T(1,128)} %bitcast.8, f32[16,4096]{1,0:T(8,128)} %weights_hbm.1, bf16[4096,256]{1,0:T(8,128)(2,1)} %centres_hbm.1), custom_call_target="tpu_custom_call" | custom-call | tf_op jit(solution)/shard_map/pallas_call | solution.py:220
  27.1 1.3 %shard_map.87 = (f32[8,16]{1,0:T(8,128)}, f32[16,64]{1,0:T(8,128)}) custom-call(f32[8,16]{1,0:T(8,128)} %get-tuple-element.6.res_in, f32[16,64]{1,0:T(8,128)} %get-tuple-element.7.corr_in), custom_call_target="tpu_custom_call" | custom-call | tf_op jit(solution)/shard_map/pallas_call | solution.py:257

commit v3 on v2

--- a/solution.py
+++ b/solution.py
@@ -28,7 +28,7 @@
     nx, ny,
     bidx, nidx, targets, eig, scales, weights_hbm, centres_hbm,
     res_out, corr_out,
-    cen, wv, w2, nj, rows_buf, rowsm, nb, acc, khi, klo,
+    cen, wv, w2, nj, rows_buf, rowsm, nb, acc, khi,
     mt_loc, mt_recv, mt_all, p_loc, p_recv, r_all,
     cen_sem, w_sem, send_sems, recv_sems,
 ):
@@ -42,7 +42,7 @@
     lanes = per * outputs
     block = eig.shape[0]
     step_j = khi.shape[1]
-    step_b = khi.shape[0]
+    step_b = khi.shape[0] // 2
     rate = -math.log2(math.e) / float(dim) ** 0.5
 
     cen_copies = []
@@ -161,10 +161,11 @@
                 norm = jnp.concatenate([nb[at_b, :]] * (256 // nb.shape[1]), axis=1)
                 tile = kern(nt(rowsm[at_b, :], cen[at, :]) + (norm + nj[:1, at]))
                 high, low = split(tile)
-                khi[:, sub * 256:(sub + 1) * 256] = high
-                klo[:, sub * 256:(sub + 1) * 256] = low
+                khi[:step_b, sub * 256:(sub + 1) * 256] = high
+                khi[step_b:, sub * 256:(sub + 1) * 256] = low
             at = pl.ds(pl.multiple_of(ji * step_j, step_j), step_j)
-            acc[at_b, :] += nt(khi[...], w2[:, at]) + nt(klo[...], w2[:, at])
+            terms = nt(khi[...], w2[:, at])
+            acc[at_b, :] += terms[:step_b] + terms[step_b:]
             return carry
 
         return lax.fori_loop(0, count // step_j, main_j, carry)
@@ -213,7 +214,7 @@
     eigen = eigvecs.shape[1]
     lanes = per * outputs
     batch = n * per
-    step_j = min(count, 1024)
+    step_j = min(count, 4096)
     step_b = min(batch, 256)
     vmem = pl.BlockSpec(memory_space=pltpu.VMEM)
     hbm = pl.BlockSpec(memory_space=pl.ANY)
@@ -234,8 +235,7 @@
             pltpu.VMEM((batch, dim), BF16),
             pltpu.VMEM((batch, 128), F32),
             pltpu.VMEM((batch, 2 * lanes), F32),
-            pltpu.VMEM((step_b, step_j), BF16),
-            pltpu.VMEM((step_b, step_j), BF16),
+            pltpu.VMEM((2 * step_b, step_j), BF16),
             pltpu.VMEM((n, per, eigen), F32),
             pltpu.VMEM((n, per, eigen), F32),
             pltpu.VMEM((n, per, eigen), F32),

time: 28.7 us -> 28 us (0.976)
  Pallas kernels: 27.8 us -> 27.2 us
    pallas_call x1, Pallas kernels: 26.5 us -> 25.8 us  [on_device(): pl.pallas_call(functools.partial(kernel, nx, ny), out_shape=(jax.ShapeDty...]
where the time goes in v3:
time: 28 us; the launch traced here: 27.8 us
  Pallas kernels  27.2 us (97%)
  between operations  0.64 us (2%)
    pallas_call x1, Pallas kernels, on_device(): pl.pallas_call(functools.partial(kernel, nx, ny), out_shape=(jax.ShapeDty...  25.8 us
    pallas_call x1, Pallas kernels, on_device(): pl.pallas_call(hand_out, out_shape=(jax.ShapeDtypeStruct(res.shape, F32),...  1.31 us

profile of v3, /device:TPU:0, one launch (start us, length us, event | category | flops | bytes accessed | tf_op | source)
XLA Modules:
  0.0 27.8 jit_solution(6388885445474902400)
XLA Ops:
  0.6 25.8 %shard_map.86 = (f32[8,16]{1,0:T(8,128)}, f32[16,64]{1,0:T(8,128)}) custom-call(s32[1,8]{1,0:T(1,128)} %bitcast.6, s32[1,64]{1,0:T(1,128)} %bitcast.7, f32[8,16]{1,0:T(8,128)} %bitcast.5, f32[64,128]{1,0:T(8,128)} %eig.1, f32[1,128]{1,0:T(1,128)} %bitcast.8, f32[16,4096]{1,0:T(8,128)} %weights_hbm.1, bf16[4096,256]{1,0:T(8,128)(2,1)} %centres_hbm.1), custom_call_target="tpu_custom_call" | custom-call | tf_op jit(solution)/shard_map/pallas_call | solution.py:221
  26.5 1.3 %shard_map.87 = (f32[8,16]{1,0:T(8,128)}, f32[16,64]{1,0:T(8,128)}) custom-call(f32[8,16]{1,0:T(8,128)} %get-tuple-element.6.res_in, f32[16,64]{1,0:T(8,128)} %get-tuple-element.7.corr_in), custom_call_target="tpu_custom_call" | custom-call | tf_op jit(solution)/shard_map/pallas_call | solution.py:257
